TPU v7x, 256 devices: a whole 4x4x8 slice. The times are simulated.
256 devices in a mesh: frame: 32 (over z_hi, y, x), head: 8 (over z_lo, core).
Axes of the slice: x: 4, y: 4, z: 8 (z_hi: 2, z_lo: 4; z = z_hi * 4 + z_lo), core: 2. Of those that a mesh axis runs over, the one named last changes fastest.
Arguments:
- queries: bfloat16 [8192, 5120], P('frame', 'head'), may hold values from -12 to 12
- keys: bfloat16 [8192, 5120], P('frame', 'head'), may hold values from -12 to 12
- values: bfloat16 [8192, 5120], P('frame', 'head'), may hold values from -6 to 6
- policy_grad: bfloat16 [8192, 5120], P('frame', 'head'), may hold values from -6 to 6
- ref_velocity: bfloat16 [8192, 5120], P('frame', 'head'), may hold values from -6 to 6
- key_lists: int32 [64, 6], P('frame'), may hold values from 0 to 63, as said below
- frame_tokens: int32 [64], replicated, may hold values from 32 to 128, as said below
Outputs:
- grad_queries: bfloat16 [8192, 5120], P('frame', 'head')
- grad_keys: bfloat16 [8192, 5120], P('frame', 'head')
- grad_values: bfloat16 [8192, 5120], P('frame', 'head')
Inputs may be any that keep to these rules, and one draw needn't show every extreme that they name: `key_lists`: row b holds 6 distinct blocks: b, the next block of the same index of frame (cyclic over its 2 blocks), and four blocks on indices of frame that differ from b's index by distinct signed powers of two. `frame_tokens`: some block is full.
All inputs are finite; a program needn't handle non-finite values.
Results may differ from a plain program's by a relative error of at most 0.011.
Values may be sent and summed in bfloat16 or wider, within the bound.
No kernel may reach another device: no remote copies, remote signals or barrier semaphores. Data moves between devices by JAX's collectives and lax.ppermute only.
A program may use at most 128 MiB of HBM per device.

v0:
```python
import math
import jax
import jax.numpy as jnp
from jax import lax
from jax.sharding import PartitionSpec as P

HEADS = 40
HD = 128
BLK = 128
kl_weight = 1.0


def from_behind(value, axis, steps):
    count = lax.axis_size(axis)
    leading, last = (max(0, -steps), min(count, count - steps))
    return lax.ppermute(value, axis, [(source, source + steps) for source in range(leading, last)])


def local(queries, keys, values, policy_grad, ref_velocity, key_lists, frame_tokens):
    rows, cols = queries.shape
    heads_here = cols // HD
    blocks_here = rows // BLK
    list_len = key_lists.shape[1]
    all_blocks = frame_tokens.shape[0]
    scale = 1.0 / math.sqrt(HD)
    levels = lax.axis_size("frame").bit_length() - 1
    me_index = lax.axis_index("frame")
    offsets = [0]
    pool_k = [keys]
    pool_v = [values]
    for level in range(levels):
        for sign in (1, -1):
            moved = from_behind((keys, values), "frame", sign * (1 << level))
            offsets.append(-sign * (1 << level))
            pool_k.append(moved[0])
            pool_v.append(moved[1])
    classes = len(offsets)
    pool_keys = jnp.stack(pool_k).reshape(classes * blocks_here, BLK, cols)
    pool_values = jnp.stack(pool_v).reshape(classes * blocks_here, BLK, cols)
    owner_gap = key_lists // blocks_here - me_index
    class_of = jnp.zeros_like(key_lists)
    for position, offset in enumerate(offsets):
        class_of = class_of + jnp.where(owner_gap == offset, position, 0)
    pool_index = class_of * blocks_here + key_lists % blocks_here
    key_block = pool_keys[pool_index].reshape(blocks_here, list_len * BLK, heads_here, HD)
    value_block = pool_values[pool_index].reshape(blocks_here, list_len * BLK, heads_here, HD)
    counts = jnp.sum(
        jnp.where(key_lists[..., None] == jnp.arange(all_blocks, dtype=jnp.int32), frame_tokens, 0),
        axis=-1,
    )
    valid = (jnp.arange(BLK, dtype=jnp.int32)[None, None, :] < counts[..., None]).reshape(
        blocks_here, list_len * BLK
    )
    query4 = queries.reshape(blocks_here, BLK, heads_here, HD)
    scores = (
        jnp.einsum("bqhd,bkhd->bhqk", query4, key_block, preferred_element_type=jnp.float32) * scale
    )
    scores = jnp.where(valid[:, None, None, :], scores, -1e30)
    highest = jnp.max(scores, axis=-1, keepdims=True)
    expd = jnp.exp(scores - highest)
    probs = expd / jnp.sum(expd, axis=-1, keepdims=True)
    probs16 = probs.astype(jnp.bfloat16)
    attn = jnp.einsum("bhqk,bkhd->bqhd", probs16, value_block, preferred_element_type=jnp.float32)
    diff = attn - ref_velocity.reshape(blocks_here, BLK, heads_here, HD).astype(jnp.float32)
    squares = lax.psum(jnp.sum(diff * diff, axis=(2, 3)), "head")
    kl = squares / (HEADS * HD)
    upstream = (
        policy_grad.reshape(blocks_here, BLK, heads_here, HD).astype(jnp.float32)
        + kl_weight * diff / (1.0 + kl)[:, :, None, None]
    )
    grad16 = upstream.astype(jnp.bfloat16)
    grad_probs = jnp.einsum(
        "bqhd,bkhd->bhqk", grad16, value_block, preferred_element_type=jnp.float32
    )
    delta = jnp.transpose(jnp.sum(grad16.astype(jnp.float32) * attn, axis=-1), (0, 2, 1))
    grad_scores16 = (probs * (grad_probs - delta[..., None])).astype(jnp.bfloat16)
    grad_q = (
        jnp.einsum("bhqk,bkhd->bqhd", grad_scores16, key_block, preferred_element_type=jnp.float32)
        * scale
    ).astype(jnp.bfloat16)
    part_k = (
        jnp.einsum("bhqk,bqhd->bkhd", grad_scores16, query4, preferred_element_type=jnp.float32)
        * scale
    )
    part_v = jnp.einsum("bhqk,bqhd->bkhd", probs16, grad16, preferred_element_type=jnp.float32)
    part_k = part_k.reshape(blocks_here * list_len, BLK * cols)
    part_v = part_v.reshape(blocks_here * list_len, BLK * cols)
    flat_index = pool_index.reshape(-1)
    selector = (
        jnp.arange(classes * blocks_here, dtype=jnp.int32)[:, None] == flat_index[None, :]
    ).astype(jnp.float32)
    pooled_k = jnp.dot(selector, part_k, precision=lax.Precision.HIGHEST).reshape(
        classes, blocks_here, BLK * cols
    )
    pooled_v = jnp.dot(selector, part_v, precision=lax.Precision.HIGHEST).reshape(
        classes, blocks_here, BLK * cols
    )
    total_k = pooled_k[0]
    total_v = pooled_v[0]
    for position in range(1, classes):
        back = from_behind(
            (pooled_k[position].astype(jnp.bfloat16), pooled_v[position].astype(jnp.bfloat16)),
            "frame",
            offsets[position],
        )
        total_k = total_k + back[0].astype(jnp.float32)
        total_v = total_v + back[1].astype(jnp.float32)
    grad_queries = grad_q.reshape(rows, cols)
    grad_keys = total_k.reshape(rows, cols).astype(jnp.bfloat16)
    grad_values = total_v.reshape(rows, cols).astype(jnp.bfloat16)
    return (grad_queries, grad_keys, grad_values)


def solution(mesh):
    in_specs = (
        P("frame", "head"),
        P("frame", "head"),
        P("frame", "head"),
        P("frame", "head"),
        P("frame", "head"),
        P("frame", None),
        P(),
    )
    out_specs = (P("frame", "head"), P("frame", "head"), P("frame", "head"))
    return jax.shard_map(local, mesh=mesh, in_specs=in_specs, out_specs=out_specs, check_vma=False)
```

profile of v0, /device:TPU:94, one launch (start us, length us, event | category | flops | bytes accessed | tf_op | source)
XLA Modules:
  0.0 415.7 jit_solution(6033962399658650368)
XLA Ops:
  0.7 7.0 %collective-permute-start = (bf16[256,640]{1,0:T(8,128)(2,1)}, bf16[256,640]{1,0:T(8,128)(2,1)}, u32[]{:S(2)}, u32[]{:S(2)}) collective-permute-start(bf16[256,640]{1,0:T(8,128)(2,1)} %param.8), channel_id=1, source_target_pairs={{0,8},{8,16},{16,24},{24,32},{32,40},{40,48},{48,56},{56,64},{64,7... | collective-permute-start | bytes 983048 | tf_op jit(solution)/shard_map/ppermute | solution.py:16
  9.6 4.9 %collective-permute-start.2 = (bf16[256,640]{1,0:T(8,128)(2,1)}, bf16[256,640]{1,0:T(8,128)(2,1)}, u32[]{:S(2)}, u32[]{:S(2)}) collective-permute-start(bf16[256,640]{1,0:T(8,128)(2,1)} %param.8), channel_id=1, source_target_pairs={{0,16},{8,24},{16,32},{24,40},{32,48},{40,56},{48,64},{56,72},{64,... | collective-permute-start | bytes 983048 | tf_op jit(solution)/shard_map/ppermute | solution.py:16
  14.5 2.5 collective-permute-start.3
  17.0 4.0 collective-permute-start.4
  29.1 8.1 %collective-permute-done = bf16[256,640]{1,0:T(8,128)(2,1)} collective-permute-done((bf16[256,640]{1,0:T(8,128)(2,1)}, bf16[256,640]{1,0:T(8,128)(2,1)}, u32[]{:S(2)}, u32[]{:S(2)}) %collective-permute-start) | collective-permute-done | bytes 327712 | tf_op jit(solution)/shard_map/ppermute | solution.py:16
  40.8 2.2 collective-permute-done.1
  46.7 11.4 %collective-permute-done.2 = bf16[256,640]{1,0:T(8,128)(2,1)} collective-permute-done((bf16[256,640]{1,0:T(8,128)(2,1)}, bf16[256,640]{1,0:T(8,128)(2,1)}, u32[]{:S(2)}, u32[]{:S(2)}) %collective-permute-start.2) | collective-permute-done | bytes 327712 | tf_op jit(solution)/shard_map/ppermute | solution.py:16
  64.8 2.8 collective-permute-done.4
  70.6 15.9 %collective-permute-start.10 = (bf16[256,640]{1,0:T(8,128)(2,1)S(1)}, bf16[256,640]{1,0:T(8,128)(2,1)S(1)}, u32[]{:S(2)}, u32[]{:S(2)}) collective-permute-start(bf16[256,640]{1,0:T(8,128)(2,1)S(1)} %copy-done.18), channel_id=1, source_target_pairs={{0,8},{8,16},{16,24},{24,32},{32,40},{40,48},{48,56},{56,64},{64,7... | collective-permute-start | bytes 983048 | tf_op jit(solution)/shard_map/ppermute | solution.py:16
  90.0 7.6 %collective-permute-start.12 = (bf16[256,640]{1,0:T(8,128)(2,1)S(1)}, bf16[256,640]{1,0:T(8,128)(2,1)S(1)}, u32[]{:S(2)}, u32[]{:S(2)}) collective-permute-start(bf16[256,640]{1,0:T(8,128)(2,1)S(1)} %copy-done.18), channel_id=1, source_target_pairs={{0,16},{8,24},{16,32},{24,40},{32,48},{40,56},{48,64},{56,72},{64,... | collective-permute-start | bytes 983048 | tf_op jit(solution)/shard_map/ppermute | solution.py:16
  101.0 2.5 collective-permute-start.14
  104.3 24.1 %collective-permute-done.10 = bf16[256,640]{1,0:T(8,128)(2,1)S(1)} collective-permute-done((bf16[256,640]{1,0:T(8,128)(2,1)S(1)}, bf16[256,640]{1,0:T(8,128)(2,1)S(1)}, u32[]{:S(2)}, u32[]{:S(2)}) %collective-permute-start.10) | collective-permute-done | bytes 327712 | tf_op jit(solution)/shard_map/ppermute | solution.py:16
  133.7 2.3 collective-permute-done.12
  136.0 3.1 collective-permute-start.17
  142.7 4.5 %collective-permute-done.14 = bf16[256,640]{1,0:T(8,128)(2,1)S(1)} collective-permute-done((bf16[256,640]{1,0:T(8,128)(2,1)S(1)}, bf16[256,640]{1,0:T(8,128)(2,1)S(1)}, u32[]{:S(2)}, u32[]{:S(2)}) %collective-permute-start.14) | collective-permute-done | bytes 327712 | tf_op jit(solution)/shard_map/ppermute | solution.py:16
  149.2 3.0 collective-permute-done.15
  153.0 3.8 collective-permute-done.16
  158.3 2.9 gather_fusion
  161.3 3.5 reshape.143
  164.8 3.5 copy.77
  171.7 4.3 %gather_fusion.1 = bf16[12,128,640]{2,1,0:T(8,128)(2,1)} fusion(bf16[22,128,640]{2,1,0:T(8,128)(2,1)} %bitcast.86, s32[1024]{0:T(1024)S(1)} %pad_clamp_fusion), kind=kCustom, calls=%fused_computation.1 | custom fusion | bytes 3932208 | tf_op jit(solution)/shard_map/gather | solution.py:46
  175.9 5.6 %reshape.144 = bf16[2,768,5,128]{3,2,1,0:T(8,128)(2,1)} reshape(bf16[12,128,640]{2,1,0:T(8,128)(2,1)} %gather_fusion.1) | data formatting | bytes 3932160 | tf_op jit(solution)/shard_map/reshape | solution.py:46
  184.3 2.1 multiply_reduce_fusion.1
  186.5 10.3 %psum.7 = f32[2,128]{1,0:T(2,128)S(1)} all-reduce(f32[2,128]{1,0:T(2,128)S(1)} %get-tuple-element.14), channel_id=1, replica_groups=mesh['frame'=32,'head'=8] {'head'}, use_global_device_ids=true, to_apply=%region_4.5 | all-reduce | flops 256 | bytes 2048 | tf_op jit(solution)/shard_map/psum | solution.py:65
  198.2 4.9 %convolution_bitcast_fusion = f32[2,768,5,128]{1,3,2,0:T(8,128)} fusion(bf16[2,128,5,128]{1,3,2,0:T(8,128)(2,1)S(1)} %get-tuple-element.13, f32[2,5,128,768]{2,3,1,0:T(8,128)} %copy-done.21, f32[2,5,128]{2,1,0:T(8,128)S(1)} %get-tuple-element.38), kind=kOutput, calls=%fused_computation.10 | convolution fusion | flops 253624320 | bytes 8197120 | tf_op jit(solution)/shard_map/bhqk,bqhd->bkhd/dot_general | solution.py:85
  206.0 5.0 %copy.81 = f32[2,768,5,128]{3,2,1,0:T(8,128)} copy(f32[2,768,5,128]{3,1,2,0:T(8,128)S(1)} %multiply_bitcast_fusion) | data formatting | bytes 7864320 | tf_op jit(solution)/shard_map/mul | solution.py:82
  211.0 5.4 %reshape.113 = f32[12,81920]{1,0:T(8,128)} reshape(f32[2,768,5,128]{3,2,1,0:T(8,128)} %copy.81) | data formatting | bytes 7864320 | tf_op jit(solution)/shard_map/reshape | solution.py:86
  216.4 9.0 %fusion.48 = (bf16[22,81920]{1,0:T(8,128)(2,1)S(1)}, f32[22,81920]{1,0:T(8,128)}) fusion(f32[12,81920]{1,0:T(8,128)} %reshape.113, s32[12]{0:T(128)S(1)} %eq.75), kind=kOutput, calls=%fused_computation.109 | convolution fusion | flops 261325056 | bytes 14745648 | tf_op jit(solution)/shard_map/dot_general | solution.py:92
  225.4 3.8 fusion.46
  229.2 3.2 collective-permute-start.29
  233.7 16.1 %collective-permute-start.27 = (bf16[2,81920]{1,0:T(2,128)(2,1)}, bf16[2,81920]{1,0:T(2,128)(2,1)S(1)}, u32[]{:S(2)}, u32[]{:S(2)}) collective-permute-start(bf16[2,81920]{1,0:T(2,128)(2,1)} %get-tuple-element.31), channel_id=1, source_target_pairs={{0,64},{8,72},{16,80},{24,88},{32,96},{40,104},{48,112},{56,120},{... | collective-permute-start | bytes 983048 | tf_op jit(solution)/shard_map/ppermute | solution.py:16
  251.8 10.8 %collective-permute-start.25 = (bf16[2,81920]{1,0:T(2,128)(2,1)}, bf16[2,81920]{1,0:T(2,128)(2,1)}, u32[]{:S(2)}, u32[]{:S(2)}) collective-permute-start(bf16[2,81920]{1,0:T(2,128)(2,1)} %get-tuple-element.33), channel_id=1, source_target_pairs={{0,32},{8,40},{16,48},{24,56},{32,64},{40,72},{48,80},{56,88},{64,... | collective-permute-start | bytes 983048 | tf_op jit(solution)/shard_map/ppermute | solution.py:16
  262.5 6.0 %copy.83 = f32[2,768,5,128]{3,2,1,0:T(8,128)} copy(f32[2,768,5,128]{1,3,2,0:T(8,128)} %convolution_bitcast_fusion) | data formatting | bytes 7864320 | tf_op jit(solution)/shard_map/bhqk,bqhd->bkhd/transpose | solution.py:85
  268.5 5.3 %reshape.114 = f32[12,81920]{1,0:T(8,128)} reshape(f32[2,768,5,128]{3,2,1,0:T(8,128)} %copy.83) | data formatting | bytes 7864320 | tf_op jit(solution)/shard_map/reshape | solution.py:87
  273.9 9.1 %fusion.49 = (bf16[22,81920]{1,0:T(8,128)(2,1)S(1)}, f32[22,81920]{1,0:T(8,128)}) fusion(f32[12,81920]{1,0:T(8,128)} %reshape.114, s32[12]{0:T(128)S(1)} %eq.75), kind=kOutput, calls=%fused_computation.110 | convolution fusion | flops 261325056 | bytes 14745648 | tf_op jit(solution)/shard_map/dot_general | solution.py:95
  285.1 13.1 %collective-permute-start.23 = (bf16[2,81920]{1,0:T(2,128)(2,1)S(1)}, bf16[2,81920]{1,0:T(2,128)(2,1)S(1)}, u32[]{:S(2)}, u32[]{:S(2)}) collective-permute-start(bf16[2,81920]{1,0:T(2,128)(2,1)S(1)} %copy-done.14), channel_id=1, source_target_pairs={{0,16},{8,24},{16,32},{24,40},{32,48},{40,56},{48,64},{56,72},{64,... | collective-permute-start | bytes 983048 | tf_op jit(solution)/shard_map/ppermute | solution.py:16
  300.1 13.3 %collective-permute-start.21 = (bf16[2,81920]{1,0:T(2,128)(2,1)S(1)}, bf16[2,81920]{1,0:T(2,128)(2,1)S(1)}, u32[]{:S(2)}, u32[]{:S(2)}) collective-permute-start(bf16[2,81920]{1,0:T(2,128)(2,1)S(1)} %copy-done.12), channel_id=1, source_target_pairs={{0,8},{8,16},{16,24},{24,32},{32,40},{40,48},{48,56},{56,64},{64,7... | collective-permute-start | bytes 983048 | tf_op jit(solution)/shard_map/ppermute | solution.py:16
  315.3 3.8 fusion.45
  325.3 14.8 %collective-permute-done.21 = bf16[2,81920]{1,0:T(2,128)(2,1)S(1)} collective-permute-done((bf16[2,81920]{1,0:T(2,128)(2,1)S(1)}, bf16[2,81920]{1,0:T(2,128)(2,1)S(1)}, u32[]{:S(2)}, u32[]{:S(2)}) %collective-permute-start.21) | collective-permute-done | bytes 327712 | tf_op jit(solution)/shard_map/ppermute | solution.py:16
  345.8 9.1 %collective-permute-done.39 = bf16[2,81920]{1,0:T(2,128)(2,1)} collective-permute-done((bf16[2,81920]{1,0:T(2,128)(2,1)}, bf16[2,81920]{1,0:T(2,128)(2,1)}, u32[]{:S(2)}, u32[]{:S(2)}) %collective-permute-start.39) | collective-permute-done | bytes 327712 | tf_op jit(solution)/shard_map/ppermute | solution.py:16
  356.8 2.9 collective-permute-start.33
  359.7 9.2 %collective-permute-done.37 = bf16[2,81920]{1,0:T(2,128)(2,1)} collective-permute-done((bf16[2,81920]{1,0:T(2,128)(2,1)}, bf16[2,81920]{1,0:T(2,128)(2,1)}, u32[]{:S(2)}, u32[]{:S(2)}) %collective-permute-start.37) | collective-permute-done | bytes 327712 | tf_op jit(solution)/shard_map/ppermute | solution.py:16
  370.8 11.9 %collective-permute-start.31 = (bf16[2,81920]{1,0:T(2,128)(2,1)}, bf16[2,81920]{1,0:T(2,128)(2,1)S(1)}, u32[]{:S(2)}, u32[]{:S(2)}) collective-permute-start(bf16[2,81920]{1,0:T(2,128)(2,1)} %get-tuple-element.27), channel_id=1, source_target_pairs={{0,8},{8,16},{16,24},{24,32},{32,40},{40,48},{48,56},{56,64},{64,7... | collective-permute-start | bytes 983048 | tf_op jit(solution)/shard_map/ppermute | solution.py:16
  382.8 2.2 collective-permute-start.30
  384.9 4.1 add_convert_fusion.1
  390.0 5.5 %collective-permute-done.31 = bf16[2,81920]{1,0:T(2,128)(2,1)S(1)} collective-permute-done((bf16[2,81920]{1,0:T(2,128)(2,1)}, bf16[2,81920]{1,0:T(2,128)(2,1)S(1)}, u32[]{:S(2)}, u32[]{:S(2)}) %collective-permute-start.31) | collective-permute-done | bytes 327712 | tf_op jit(solution)/shard_map/ppermute | solution.py:16
  395.5 15.2 %collective-permute-done.30 = bf16[2,81920]{1,0:T(2,128)(2,1)S(1)} collective-permute-done((bf16[2,81920]{1,0:T(2,128)(2,1)}, bf16[2,81920]{1,0:T(2,128)(2,1)S(1)}, u32[]{:S(2)}, u32[]{:S(2)}) %collective-permute-start.30) | collective-permute-done | bytes 327712 | tf_op jit(solution)/shard_map/ppermute | solution.py:16
  410.7 4.0 add_convert_fusion
  (144 shorter events, 84.8 us)
Async XLA Ops:
  0.6 26.1 %copy-start.18 = (bf16[256,640]{1,0:T(8,128)(2,1)S(1)}, bf16[256,640]{1,0:T(8,128)(2,1)}, u32[]{:S(2)}) copy-start(bf16[256,640]{1,0:T(8,128)(2,1)} %param.9) | copy-start | bytes 983044
  0.6 26.9 %copy-start.16 = (bf16[256,640]{1,0:T(8,128)(2,1)S(1)}, bf16[256,640]{1,0:T(8,128)(2,1)}, u32[]{:S(2)}) copy-start(bf16[256,640]{1,0:T(8,128)(2,1)} %param.7) | copy-start | bytes 983044
  0.7 27.3 %copy-start.20 = (s32[64]{0:T(128)S(1)}, s32[64]{0:T(128)}, u32[]{:S(2)}) copy-start(s32[64]{0:T(128)} %param.13) | copy-start | bytes 772
  0.7 27.7 %copy-start.19 = (bf16[256,640]{1,0:T(8,128)(2,1)S(1)}, bf16[256,640]{1,0:T(8,128)(2,1)}, u32[]{:S(2)}) copy-start(bf16[256,640]{1,0:T(8,128)(2,1)} %param.10) | copy-start | bytes 983044
  0.7 36.5 %collective-permute-start = (bf16[256,640]{1,0:T(8,128)(2,1)}, bf16[256,640]{1,0:T(8,128)(2,1)}, u32[]{:S(2)}, u32[]{:S(2)}) collective-permute-start(bf16[256,640]{1,0:T(8,128)(2,1)} %param.8), channel_id=1, source_target_pairs={{0,8},{8,16},{16,24},{24,32},{32,40},{40,48},{48,56},{56,64},{64,7... | collective-permute-start | bytes 983048 | tf_op jit(solution)/shard_map/ppermute | solution.py:16
  7.7 35.3 %collective-permute-start.1 = (bf16[256,640]{1,0:T(8,128)(2,1)}, bf16[256,640]{1,0:T(8,128)(2,1)}, u32[]{:S(2)}, u32[]{:S(2)}) collective-permute-start(bf16[256,640]{1,0:T(8,128)(2,1)} %param.8), channel_id=1, source_target_pairs={{8,0},{16,8},{24,16},{32,24},{40,32},{48,40},{56,48},{64,56},{72,6... | collective-permute-start | bytes 983048 | tf_op jit(solution)/shard_map/ppermute | solution.py:16
  9.6 48.4 %collective-permute-start.2 = (bf16[256,640]{1,0:T(8,128)(2,1)}, bf16[256,640]{1,0:T(8,128)(2,1)}, u32[]{:S(2)}, u32[]{:S(2)}) collective-permute-start(bf16[256,640]{1,0:T(8,128)(2,1)} %param.8), channel_id=1, source_target_pairs={{0,16},{8,24},{16,32},{24,40},{32,48},{40,56},{48,64},{56,72},{64,... | collective-permute-start | bytes 983048 | tf_op jit(solution)/shard_map/ppermute | solution.py:16
  14.5 47.3 %collective-permute-start.3 = (bf16[256,640]{1,0:T(8,128)(2,1)}, bf16[256,640]{1,0:T(8,128)(2,1)}, u32[]{:S(2)}, u32[]{:S(2)}) collective-permute-start(bf16[256,640]{1,0:T(8,128)(2,1)} %param.8), channel_id=1, source_target_pairs={{16,0},{24,8},{32,16},{40,24},{48,32},{56,40},{64,48},{72,56},{80,... | collective-permute-start | bytes 983048 | tf_op jit(solution)/shard_map/ppermute | solution.py:16
  17.0 50.6 %collective-permute-start.4 = (bf16[256,640]{1,0:T(8,128)(2,1)}, bf16[256,640]{1,0:T(8,128)(2,1)}, u32[]{:S(2)}, u32[]{:S(2)}) collective-permute-start(bf16[256,640]{1,0:T(8,128)(2,1)} %param.8), channel_id=1, source_target_pairs={{0,32},{8,40},{16,48},{24,56},{32,64},{40,72},{48,80},{56,88},{64,... | collective-permute-start | bytes 983048 | tf_op jit(solution)/shard_map/ppermute | solution.py:16
  37.1 33.4 %collective-permute-start.5 = (bf16[256,640]{1,0:T(8,128)(2,1)S(1)}, bf16[256,640]{1,0:T(8,128)(2,1)S(1)}, u32[]{:S(2)}, u32[]{:S(2)}) collective-permute-start(bf16[256,640]{1,0:T(8,128)(2,1)S(1)} %copy-done.17), channel_id=1, source_target_pairs={{32,0},{40,8},{48,16},{56,24},{64,32},{72,40},{80,48},{88,56},{96,... | collective-permute-start | bytes 983048 | tf_op jit(solution)/shard_map/ppermute | solution.py:16
  43.0 44.3 %collective-permute-start.6 = (bf16[256,640]{1,0:T(8,128)(2,1)S(1)}, bf16[256,640]{1,0:T(8,128)(2,1)S(1)}, u32[]{:S(2)}, u32[]{:S(2)}) collective-permute-start(bf16[256,640]{1,0:T(8,128)(2,1)S(1)} %copy-done.17), channel_id=1, source_target_pairs={{0,64},{8,72},{16,80},{24,88},{32,96},{40,104},{48,112},{56,120},{... | collective-permute-start | bytes 983048 | tf_op jit(solution)/shard_map/ppermute | solution.py:16
  58.1 31.9 %collective-permute-start.7 = (bf16[256,640]{1,0:T(8,128)(2,1)S(1)}, bf16[256,640]{1,0:T(8,128)(2,1)S(1)}, u32[]{:S(2)}, u32[]{:S(2)}) collective-permute-start(bf16[256,640]{1,0:T(8,128)(2,1)S(1)} %copy-done.17), channel_id=1, source_target_pairs={{64,0},{72,8},{80,16},{88,24},{96,32},{104,40},{112,48},{120,56},{... | collective-permute-start | bytes 983048 | tf_op jit(solution)/shard_map/ppermute | solution.py:16
  61.7 36.6 %collective-permute-start.8 = (bf16[256,640]{1,0:T(8,128)(2,1)S(1)}, bf16[256,640]{1,0:T(8,128)(2,1)S(1)}, u32[]{:S(2)}, u32[]{:S(2)}) collective-permute-start(bf16[256,640]{1,0:T(8,128)(2,1)S(1)} %copy-done.17), channel_id=1, source_target_pairs={{0,128},{8,136},{16,144},{24,152},{32,160},{40,168},{48,176},{56,1... | collective-permute-start | bytes 983048 | tf_op jit(solution)/shard_map/ppermute | solution.py:16
  67.5 33.5 %collective-permute-start.9 = (bf16[256,640]{1,0:T(8,128)(2,1)S(1)}, bf16[256,640]{1,0:T(8,128)(2,1)S(1)}, u32[]{:S(2)}, u32[]{:S(2)}) collective-permute-start(bf16[256,640]{1,0:T(8,128)(2,1)S(1)} %copy-done.17), channel_id=1, source_target_pairs={{128,0},{136,8},{144,16},{152,24},{160,32},{168,40},{176,48},{184,... | collective-permute-start | bytes 983048 | tf_op jit(solution)/shard_map/ppermute | solution.py:16
  70.6 57.8 %collective-permute-start.10 = (bf16[256,640]{1,0:T(8,128)(2,1)S(1)}, bf16[256,640]{1,0:T(8,128)(2,1)S(1)}, u32[]{:S(2)}, u32[]{:S(2)}) collective-permute-start(bf16[256,640]{1,0:T(8,128)(2,1)S(1)} %copy-done.18), channel_id=1, source_target_pairs={{0,8},{8,16},{16,24},{24,32},{32,40},{40,48},{48,56},{56,64},{64,7... | collective-permute-start | bytes 983048 | tf_op jit(solution)/shard_map/ppermute | solution.py:16
  87.3 43.8 %collective-permute-start.11 = (bf16[256,640]{1,0:T(8,128)(2,1)S(1)}, bf16[256,640]{1,0:T(8,128)(2,1)S(1)}, u32[]{:S(2)}, u32[]{:S(2)}) collective-permute-start(bf16[256,640]{1,0:T(8,128)(2,1)S(1)} %copy-done.18), channel_id=1, source_target_pairs={{8,0},{16,8},{24,16},{32,24},{40,32},{48,40},{56,48},{64,56},{72,6... | collective-permute-start | bytes 983048 | tf_op jit(solution)/shard_map/ppermute | solution.py:16
  90.0 46.1 %collective-permute-start.12 = (bf16[256,640]{1,0:T(8,128)(2,1)S(1)}, bf16[256,640]{1,0:T(8,128)(2,1)S(1)}, u32[]{:S(2)}, u32[]{:S(2)}) collective-permute-start(bf16[256,640]{1,0:T(8,128)(2,1)S(1)} %copy-done.18), channel_id=1, source_target_pairs={{0,16},{8,24},{16,32},{24,40},{32,48},{40,56},{48,64},{56,72},{64,... | collective-permute-start | bytes 983048 | tf_op jit(solution)/shard_map/ppermute | solution.py:16
  98.4 41.5 %collective-permute-start.13 = (bf16[256,640]{1,0:T(8,128)(2,1)S(1)}, bf16[256,640]{1,0:T(8,128)(2,1)S(1)}, u32[]{:S(2)}, u32[]{:S(2)}) collective-permute-start(bf16[256,640]{1,0:T(8,128)(2,1)S(1)} %copy-done.18), channel_id=1, source_target_pairs={{16,0},{24,8},{32,16},{40,24},{48,32},{56,40},{64,48},{72,56},{80,... | collective-permute-start | bytes 983048 | tf_op jit(solution)/shard_map/ppermute | solution.py:16
  101.0 46.2 %collective-permute-start.14 = (bf16[256,640]{1,0:T(8,128)(2,1)S(1)}, bf16[256,640]{1,0:T(8,128)(2,1)S(1)}, u32[]{:S(2)}, u32[]{:S(2)}) collective-permute-start(bf16[256,640]{1,0:T(8,128)(2,1)S(1)} %copy-done.18), channel_id=1, source_target_pairs={{0,32},{8,40},{16,48},{24,56},{32,64},{40,72},{48,80},{56,88},{64,... | collective-permute-start | bytes 983048 | tf_op jit(solution)/shard_map/ppermute | solution.py:16
  128.3 23.9 %collective-permute-start.15 = (bf16[256,640]{1,0:T(8,128)(2,1)S(1)}, bf16[256,640]{1,0:T(8,128)(2,1)S(1)}, u32[]{:S(2)}, u32[]{:S(2)}) collective-permute-start(bf16[256,640]{1,0:T(8,128)(2,1)S(1)} %copy-done.18), channel_id=1, source_target_pairs={{32,0},{40,8},{48,16},{56,24},{64,32},{72,40},{80,48},{88,56},{96,... | collective-permute-start | bytes 983048 | tf_op jit(solution)/shard_map/ppermute | solution.py:16
  131.0 25.8 %collective-permute-start.16 = (bf16[256,640]{1,0:T(8,128)(2,1)S(1)}, bf16[256,640]{1,0:T(8,128)(2,1)S(1)}, u32[]{:S(2)}, u32[]{:S(2)}) collective-permute-start(bf16[256,640]{1,0:T(8,128)(2,1)S(1)} %copy-done.18), channel_id=1, source_target_pairs={{0,64},{8,72},{16,80},{24,88},{32,96},{40,104},{48,112},{56,120},{... | collective-permute-start | bytes 983048 | tf_op jit(solution)/shard_map/ppermute | solution.py:16
  136.0 21.5 %collective-permute-start.17 = (bf16[256,640]{1,0:T(8,128)(2,1)S(1)}, bf16[256,640]{1,0:T(8,128)(2,1)S(1)}, u32[]{:S(2)}, u32[]{:S(2)}) collective-permute-start(bf16[256,640]{1,0:T(8,128)(2,1)S(1)} %copy-done.18), channel_id=1, source_target_pairs={{64,0},{72,8},{80,16},{88,24},{96,32},{104,40},{112,48},{120,56},{... | collective-permute-start | bytes 983048 | tf_op jit(solution)/shard_map/ppermute | solution.py:16
  139.9 28.3 %collective-permute-start.18 = (bf16[256,640]{1,0:T(8,128)(2,1)S(1)}, bf16[256,640]{1,0:T(8,128)(2,1)}, u32[]{:S(2)}, u32[]{:S(2)}) collective-permute-start(bf16[256,640]{1,0:T(8,128)(2,1)S(1)} %copy-done.18), channel_id=1, source_target_pairs={{0,128},{8,136},{16,144},{24,152},{32,160},{40,168},{48,176},{56,1... | collective-permute-start | bytes 983048 | tf_op jit(solution)/shard_map/ppermute | solution.py:16
  147.2 22.8 %collective-permute-start.19 = (bf16[256,640]{1,0:T(8,128)(2,1)S(1)}, bf16[256,640]{1,0:T(8,128)(2,1)}, u32[]{:S(2)}, u32[]{:S(2)}) collective-permute-start(bf16[256,640]{1,0:T(8,128)(2,1)S(1)} %copy-done.18), channel_id=1, source_target_pairs={{128,0},{136,8},{144,16},{152,24},{160,32},{168,40},{176,48},{184,... | collective-permute-start | bytes 983048 | tf_op jit(solution)/shard_map/ppermute | solution.py:16
  229.2 53.8 %collective-permute-start.29 = (bf16[2,81920]{1,0:T(2,128)(2,1)}, bf16[2,81920]{1,0:T(2,128)(2,1)S(1)}, u32[]{:S(2)}, u32[]{:S(2)}) collective-permute-start(bf16[2,81920]{1,0:T(2,128)(2,1)} %get-tuple-element.29), channel_id=1, source_target_pairs={{0,128},{8,136},{16,144},{24,152},{32,160},{40,168},{48,176},{56,1... | collective-permute-start | bytes 983048 | tf_op jit(solution)/shard_map/ppermute | solution.py:16
  232.4 52.7 %collective-permute-start.28 = (bf16[2,81920]{1,0:T(2,128)(2,1)}, bf16[2,81920]{1,0:T(2,128)(2,1)S(1)}, u32[]{:S(2)}, u32[]{:S(2)}) collective-permute-start(bf16[2,81920]{1,0:T(2,128)(2,1)} %get-tuple-element.30), channel_id=1, source_target_pairs={{128,0},{136,8},{144,16},{152,24},{160,32},{168,40},{176,48},{184,... | collective-permute-start | bytes 983048 | tf_op jit(solution)/shard_map/ppermute | solution.py:16
  233.7 64.5 %collective-permute-start.27 = (bf16[2,81920]{1,0:T(2,128)(2,1)}, bf16[2,81920]{1,0:T(2,128)(2,1)S(1)}, u32[]{:S(2)}, u32[]{:S(2)}) collective-permute-start(bf16[2,81920]{1,0:T(2,128)(2,1)} %get-tuple-element.31), channel_id=1, source_target_pairs={{0,64},{8,72},{16,80},{24,88},{32,96},{40,104},{48,112},{56,120},{... | collective-permute-start | bytes 983048 | tf_op jit(solution)/shard_map/ppermute | solution.py:16
  249.8 50.2 %collective-permute-start.26 = (bf16[2,81920]{1,0:T(2,128)(2,1)}, bf16[2,81920]{1,0:T(2,128)(2,1)S(1)}, u32[]{:S(2)}, u32[]{:S(2)}) collective-permute-start(bf16[2,81920]{1,0:T(2,128)(2,1)} %get-tuple-element.32), channel_id=1, source_target_pairs={{64,0},{72,8},{80,16},{88,24},{96,32},{104,40},{112,48},{120,56},{... | collective-permute-start | bytes 983048 | tf_op jit(solution)/shard_map/ppermute | solution.py:16
  251.8 61.6 %collective-permute-start.25 = (bf16[2,81920]{1,0:T(2,128)(2,1)}, bf16[2,81920]{1,0:T(2,128)(2,1)}, u32[]{:S(2)}, u32[]{:S(2)}) collective-permute-start(bf16[2,81920]{1,0:T(2,128)(2,1)} %get-tuple-element.33), channel_id=1, source_target_pairs={{0,32},{8,40},{16,48},{24,56},{32,64},{40,72},{48,80},{56,88},{64,... | collective-permute-start | bytes 983048 | tf_op jit(solution)/shard_map/ppermute | solution.py:16
  273.9 26.2 %copy-start.12 = (bf16[2,81920]{1,0:T(2,128)(2,1)S(1)}, bf16[2,81920]{1,0:T(2,128)(2,1)}, u32[]{:S(2)}) copy-start(bf16[2,81920]{1,0:T(2,128)(2,1)} %get-tuple-element.37) | copy-start | bytes 983044
  273.9 39.5 %copy-start.10 = (bf16[2,81920]{1,0:T(2,128)(2,1)S(1)}, bf16[2,81920]{1,0:T(2,128)(2,1)}, u32[]{:S(2)}) copy-start(bf16[2,81920]{1,0:T(2,128)(2,1)} %get-tuple-element.28) | copy-start | bytes 983044
  283.0 61.0 %copy-start.1 = (bf16[2,5,128,768]{2,3,1,0:T(8,128)(2,1)S(1)}, bf16[2,5,128,768]{2,3,1,0:T(8,128)(2,1)}, u32[]{:S(2)}) copy-start(bf16[2,5,128,768]{2,3,1,0:T(8,128)(2,1)} %copy-done) | copy-start | bytes 5898244
  283.0 36.2 %collective-permute-start.24 = (bf16[2,81920]{1,0:T(2,128)(2,1)S(1)}, bf16[2,81920]{1,0:T(2,128)(2,1)S(1)}, u32[]{:S(2)}, u32[]{:S(2)}) collective-permute-start(bf16[2,81920]{1,0:T(2,128)(2,1)S(1)} %copy-done.15), channel_id=1, source_target_pairs={{32,0},{40,8},{48,16},{56,24},{64,32},{72,40},{80,48},{88,56},{96,... | collective-permute-start | bytes 983048 | tf_op jit(solution)/shard_map/ppermute | solution.py:16
  285.1 36.1 %collective-permute-start.23 = (bf16[2,81920]{1,0:T(2,128)(2,1)S(1)}, bf16[2,81920]{1,0:T(2,128)(2,1)S(1)}, u32[]{:S(2)}, u32[]{:S(2)}) collective-permute-start(bf16[2,81920]{1,0:T(2,128)(2,1)S(1)} %copy-done.14), channel_id=1, source_target_pairs={{0,16},{8,24},{16,32},{24,40},{32,48},{40,56},{48,64},{56,72},{64,... | collective-permute-start | bytes 983048 | tf_op jit(solution)/shard_map/ppermute | solution.py:16
  298.1 25.2 %collective-permute-start.22 = (bf16[2,81920]{1,0:T(2,128)(2,1)S(1)}, bf16[2,81920]{1,0:T(2,128)(2,1)S(1)}, u32[]{:S(2)}, u32[]{:S(2)}) collective-permute-start(bf16[2,81920]{1,0:T(2,128)(2,1)S(1)} %copy-done.13), channel_id=1, source_target_pairs={{16,0},{24,8},{32,16},{40,24},{48,32},{56,40},{64,48},{72,56},{80,... | collective-permute-start | bytes 983048 | tf_op jit(solution)/shard_map/ppermute | solution.py:16
  300.1 41.9 %copy-start.5 = (bf16[2,81920]{1,0:T(2,128)(2,1)}, bf16[2,81920]{1,0:T(2,128)(2,1)S(1)}, u32[]{:S(2)}) copy-start(bf16[2,81920]{1,0:T(2,128)(2,1)S(1)} %collective-permute-done.26) | copy-start | bytes 983044
  300.1 40.0 %collective-permute-start.21 = (bf16[2,81920]{1,0:T(2,128)(2,1)S(1)}, bf16[2,81920]{1,0:T(2,128)(2,1)S(1)}, u32[]{:S(2)}, u32[]{:S(2)}) collective-permute-start(bf16[2,81920]{1,0:T(2,128)(2,1)S(1)} %copy-done.12), channel_id=1, source_target_pairs={{0,8},{8,16},{16,24},{24,32},{32,40},{40,48},{48,56},{56,64},{64,7... | collective-permute-start | bytes 983048 | tf_op jit(solution)/shard_map/ppermute | solution.py:16
  313.4 28.6 %collective-permute-start.20 = (bf16[2,81920]{1,0:T(2,128)(2,1)S(1)}, bf16[2,81920]{1,0:T(2,128)(2,1)S(1)}, u32[]{:S(2)}, u32[]{:S(2)}) collective-permute-start(bf16[2,81920]{1,0:T(2,128)(2,1)S(1)} %copy-done.10), channel_id=1, source_target_pairs={{8,0},{16,8},{24,16},{32,24},{40,32},{48,40},{56,48},{64,56},{72,6... | collective-permute-start | bytes 983048 | tf_op jit(solution)/shard_map/ppermute | solution.py:16
  319.2 35.7 %collective-permute-start.39 = (bf16[2,81920]{1,0:T(2,128)(2,1)}, bf16[2,81920]{1,0:T(2,128)(2,1)}, u32[]{:S(2)}, u32[]{:S(2)}) collective-permute-start(bf16[2,81920]{1,0:T(2,128)(2,1)} %get-tuple-element.19), channel_id=1, source_target_pairs={{0,128},{8,136},{16,144},{24,152},{32,160},{40,168},{48,176},{56,1... | collective-permute-start | bytes 983048 | tf_op jit(solution)/shard_map/ppermute | solution.py:16
  321.2 35.6 %collective-permute-start.38 = (bf16[2,81920]{1,0:T(2,128)(2,1)}, bf16[2,81920]{1,0:T(2,128)(2,1)}, u32[]{:S(2)}, u32[]{:S(2)}) collective-permute-start(bf16[2,81920]{1,0:T(2,128)(2,1)} %get-tuple-element.20), channel_id=1, source_target_pairs={{128,0},{136,8},{144,16},{152,24},{160,32},{168,40},{176,48},{184,... | collective-permute-start | bytes 983048 | tf_op jit(solution)/shard_map/ppermute | solution.py:16
  323.4 45.5 %collective-permute-start.37 = (bf16[2,81920]{1,0:T(2,128)(2,1)}, bf16[2,81920]{1,0:T(2,128)(2,1)}, u32[]{:S(2)}, u32[]{:S(2)}) collective-permute-start(bf16[2,81920]{1,0:T(2,128)(2,1)} %get-tuple-element.21), channel_id=1, source_target_pairs={{0,64},{8,72},{16,80},{24,88},{32,96},{40,104},{48,112},{56,120},{... | collective-permute-start | bytes 983048 | tf_op jit(solution)/shard_map/ppermute | solution.py:16
  340.1 30.7 %collective-permute-start.36 = (bf16[2,81920]{1,0:T(2,128)(2,1)}, bf16[2,81920]{1,0:T(2,128)(2,1)}, u32[]{:S(2)}, u32[]{:S(2)}) collective-permute-start(bf16[2,81920]{1,0:T(2,128)(2,1)} %get-tuple-element.22), channel_id=1, source_target_pairs={{64,0},{72,8},{80,16},{88,24},{96,32},{104,40},{112,48},{120,56},{... | collective-permute-start | bytes 983048 | tf_op jit(solution)/shard_map/ppermute | solution.py:16
  342.0 40.7 %collective-permute-start.35 = (bf16[2,81920]{1,0:T(2,128)(2,1)}, bf16[2,81920]{1,0:T(2,128)(2,1)}, u32[]{:S(2)}, u32[]{:S(2)}) collective-permute-start(bf16[2,81920]{1,0:T(2,128)(2,1)} %get-tuple-element.23), channel_id=1, source_target_pairs={{0,32},{8,40},{16,48},{24,56},{32,64},{40,72},{48,80},{56,88},{64,... | collective-permute-start | bytes 983048 | tf_op jit(solution)/shard_map/ppermute | solution.py:16
  354.9 35.2 %collective-permute-start.34 = (bf16[2,81920]{1,0:T(2,128)(2,1)}, bf16[2,81920]{1,0:T(2,128)(2,1)S(1)}, u32[]{:S(2)}, u32[]{:S(2)}) collective-permute-start(bf16[2,81920]{1,0:T(2,128)(2,1)} %get-tuple-element.24), channel_id=1, source_target_pairs={{32,0},{40,8},{48,16},{56,24},{64,32},{72,40},{80,48},{88,56},{96,... | collective-permute-start | bytes 983048 | tf_op jit(solution)/shard_map/ppermute | solution.py:16
  356.8 33.2 %collective-permute-start.33 = (bf16[2,81920]{1,0:T(2,128)(2,1)}, bf16[2,81920]{1,0:T(2,128)(2,1)S(1)}, u32[]{:S(2)}, u32[]{:S(2)}) collective-permute-start(bf16[2,81920]{1,0:T(2,128)(2,1)} %get-tuple-element.25), channel_id=1, source_target_pairs={{0,16},{8,24},{16,32},{24,40},{32,48},{40,56},{48,64},{56,72},{64,... | collective-permute-start | bytes 983048 | tf_op jit(solution)/shard_map/ppermute | solution.py:16
  368.9 21.1 %collective-permute-start.32 = (bf16[2,81920]{1,0:T(2,128)(2,1)}, bf16[2,81920]{1,0:T(2,128)(2,1)S(1)}, u32[]{:S(2)}, u32[]{:S(2)}) collective-permute-start(bf16[2,81920]{1,0:T(2,128)(2,1)} %get-tuple-element.26), channel_id=1, source_target_pairs={{16,0},{24,8},{32,16},{40,24},{48,32},{56,40},{64,48},{72,56},{80,... | collective-permute-start | bytes 983048 | tf_op jit(solution)/shard_map/ppermute | solution.py:16
  370.8 24.7 %collective-permute-start.31 = (bf16[2,81920]{1,0:T(2,128)(2,1)}, bf16[2,81920]{1,0:T(2,128)(2,1)S(1)}, u32[]{:S(2)}, u32[]{:S(2)}) collective-permute-start(bf16[2,81920]{1,0:T(2,128)(2,1)} %get-tuple-element.27), channel_id=1, source_target_pairs={{0,8},{8,16},{16,24},{24,32},{32,40},{40,48},{48,56},{56,64},{64,7... | collective-permute-start | bytes 983048 | tf_op jit(solution)/shard_map/ppermute | solution.py:16
  382.8 28.0 %collective-permute-start.30 = (bf16[2,81920]{1,0:T(2,128)(2,1)}, bf16[2,81920]{1,0:T(2,128)(2,1)S(1)}, u32[]{:S(2)}, u32[]{:S(2)}) collective-permute-start(bf16[2,81920]{1,0:T(2,128)(2,1)} %get-tuple-element.18), channel_id=1, source_target_pairs={{8,0},{16,8},{24,16},{32,24},{40,32},{48,40},{56,48},{64,56},{72,6... | collective-permute-start | bytes 983048 | tf_op jit(solution)/shard_map/ppermute | solution.py:16
  (15 other events, 149.3 us)
where the time goes:
time: 418 us; the launch traced here: 416 us
  starting transfers between devices  164 us (39%)
  waiting for transfers between devices  117 us (28%)
  local copies, waits for them, and re-layouts  82.9 us (20%)
  matrix products  28 us (7%)
  other arithmetic  12 us (3%)
  blocking collectives  10.3 us (2%)
    ppermute x40, starting transfers between devices, from_behind(): lax.ppermute(value, axis, [(source, source + steps) for source in range(l...  164 us
    ppermute x40, waiting for transfers between devices, from_behind(): lax.ppermute(value, axis, [(source, source + steps) for source in range(l...  117 us
    unnamed x70, local copies, waits for them, and re-layouts  25.8 us
    psum x1, blocking collectives, local(): squares = lax.psum(jnp.sum(diff * diff, axis=(2, 3)), 'head')  10.3 us
    dot_general x1, matrix products, local(): jnp.dot(selector, part_v, precision=lax.Precision.HIGHEST)  9.11 us
    dot_general x1, matrix products, local(): jnp.dot(selector, part_k, precision=lax.Precision.HIGHEST)  9 us
  transfers between devices with their start and end apart: 40, of which 15 were waited for; matrix products, arithmetic and copies ran while one was open for 17% of the time, Pallas kernels for 0%

commit v1 on v0

--- a/solution.py
+++ b/solution.py
@@ -1,3 +1,4 @@
+import functools
 import math
 import jax
 import jax.numpy as jnp
@@ -8,6 +9,14 @@
 HD = 128
 BLK = 128
 kl_weight = 1.0
+
+
+def set_the_roots(x_local, net_axis):
+    s_next = lax.all_gather(x_local, net_axis)
+    return jnp.sum(s_next, axis=0)
+
+
+slabs_update = functools.partial(set_the_roots, net_axis="head")
 
 
 def from_behind(value, axis, steps):
@@ -62,7 +71,7 @@
     probs16 = probs.astype(jnp.bfloat16)
     attn = jnp.einsum("bhqk,bkhd->bqhd", probs16, value_block, preferred_element_type=jnp.float32)
     diff = attn - ref_velocity.reshape(blocks_here, BLK, heads_here, HD).astype(jnp.float32)
-    squares = lax.psum(jnp.sum(diff * diff, axis=(2, 3)), "head")
+    squares = slabs_update(jnp.sum(diff * diff, axis=(2, 3)))
     kl = squares / (HEADS * HD)
     upstream = (
         policy_grad.reshape(blocks_here, BLK, heads_here, HD).astype(jnp.float32)

time: 418 us -> 416 us (level)
    psum x1 -> x0, blocking collectives: 10.3 us -> none  [local(): squares = lax.psum(jnp.sum(diff * diff, axis=(2, 3)), 'head')]
    all_gather x0 -> x1, blocking collectives: none -> 9.58 us  [set_the_roots(): s_next = lax.all_gather(x_local, net_axis)]
    ppermute x40, starting transfers between devices: 164 us -> 160 us  [from_behind(): lax.ppermute(value, axis, [(source, source + steps) for source in range(l...]
  transfers between devices with their start and end apart: 40 -> 40, of which waited for: 15 -> 17; matrix products, arithmetic and copies ran while one was open for 17% -> 17% of each run, Pallas kernels for 0% -> 0%
where the time goes in v1:
time: 416 us; the launch traced here: 413 us
  starting transfers between devices  160 us (38%)
  waiting for transfers between devices  119 us (29%)
  local copies, waits for them, and re-layouts  82.9 us (20%)
  matrix products  28 us (7%)
  other arithmetic  12.1 us (3%)
  blocking collectives  9.58 us (2%)
    ppermute x40, starting transfers between devices, from_behind(): lax.ppermute(value, axis, [(source, source + steps) for source in range(l...  160 us
    ppermute x40, waiting for transfers between devices, from_behind(): lax.ppermute(value, axis, [(source, source + steps) for source in range(l...  119 us
    unnamed x70, local copies, waits for them, and re-layouts  25.8 us
    all_gather x1, blocking collectives, set_the_roots(): s_next = lax.all_gather(x_local, net_axis)  9.58 us
    dot_general x1, matrix products, local(): jnp.dot(selector, part_v, precision=lax.Precision.HIGHEST)  9.11 us
    dot_general x1, matrix products, local(): jnp.dot(selector, part_k, precision=lax.Precision.HIGHEST)  9 us
  transfers between devices with their start and end apart: 40, of which 17 were waited for; matrix products, arithmetic and copies ran while one was open for 17% of the time, Pallas kernels for 0%

profile of v1, /device:TPU:94, one launch (start us, length us, event | category | flops | bytes accessed | tf_op | source)
XLA Modules:
  0.0 413.0 jit_solution(15818609672130254806)
XLA Ops:
  0.7 7.0 %collective-permute-start = (bf16[256,640]{1,0:T(8,128)(2,1)}, bf16[256,640]{1,0:T(8,128)(2,1)}, u32[]{:S(2)}, u32[]{:S(2)}) collective-permute-start(bf16[256,640]{1,0:T(8,128)(2,1)} %param.8), channel_id=1, source_target_pairs={{0,8},{8,16},{16,24},{24,32},{32,40},{40,48},{48,56},{56,64},{64,7... | collective-permute-start | bytes 983048 | tf_op jit(solution)/shard_map/ppermute | solution.py:25
  9.6 4.9 %collective-permute-start.2 = (bf16[256,640]{1,0:T(8,128)(2,1)}, bf16[256,640]{1,0:T(8,128)(2,1)}, u32[]{:S(2)}, u32[]{:S(2)}) collective-permute-start(bf16[256,640]{1,0:T(8,128)(2,1)} %param.8), channel_id=1, source_target_pairs={{0,16},{8,24},{16,32},{24,40},{32,48},{40,56},{48,64},{56,72},{64,... | collective-permute-start | bytes 983048 | tf_op jit(solution)/shard_map/ppermute | solution.py:25
  14.5 2.5 collective-permute-start.3
  17.0 4.0 collective-permute-start.4
  29.1 8.1 %collective-permute-done = bf16[256,640]{1,0:T(8,128)(2,1)} collective-permute-done((bf16[256,640]{1,0:T(8,128)(2,1)}, bf16[256,640]{1,0:T(8,128)(2,1)}, u32[]{:S(2)}, u32[]{:S(2)}) %collective-permute-start) | collective-permute-done | bytes 327712 | tf_op jit(solution)/shard_map/ppermute | solution.py:25
  40.8 2.2 collective-permute-done.1
  46.7 11.4 %collective-permute-done.2 = bf16[256,640]{1,0:T(8,128)(2,1)} collective-permute-done((bf16[256,640]{1,0:T(8,128)(2,1)}, bf16[256,640]{1,0:T(8,128)(2,1)}, u32[]{:S(2)}, u32[]{:S(2)}) %collective-permute-start.2) | collective-permute-done | bytes 327712 | tf_op jit(solution)/shard_map/ppermute | solution.py:25
  64.8 2.8 collective-permute-done.4
  70.6 15.9 %collective-permute-start.10 = (bf16[256,640]{1,0:T(8,128)(2,1)S(1)}, bf16[256,640]{1,0:T(8,128)(2,1)S(1)}, u32[]{:S(2)}, u32[]{:S(2)}) collective-permute-start(bf16[256,640]{1,0:T(8,128)(2,1)S(1)} %copy-done.18), channel_id=1, source_target_pairs={{0,8},{8,16},{16,24},{24,32},{32,40},{40,48},{48,56},{56,64},{64,7... | collective-permute-start | bytes 983048 | tf_op jit(solution)/shard_map/ppermute | solution.py:25
  90.0 7.6 %collective-permute-start.12 = (bf16[256,640]{1,0:T(8,128)(2,1)S(1)}, bf16[256,640]{1,0:T(8,128)(2,1)S(1)}, u32[]{:S(2)}, u32[]{:S(2)}) collective-permute-start(bf16[256,640]{1,0:T(8,128)(2,1)S(1)} %copy-done.18), channel_id=1, source_target_pairs={{0,16},{8,24},{16,32},{24,40},{32,48},{40,56},{48,64},{56,72},{64,... | collective-permute-start | bytes 983048 | tf_op jit(solution)/shard_map/ppermute | solution.py:25
  101.0 2.5 collective-permute-start.14
  104.3 24.1 %collective-permute-done.10 = bf16[256,640]{1,0:T(8,128)(2,1)S(1)} collective-permute-done((bf16[256,640]{1,0:T(8,128)(2,1)S(1)}, bf16[256,640]{1,0:T(8,128)(2,1)S(1)}, u32[]{:S(2)}, u32[]{:S(2)}) %collective-permute-start.10) | collective-permute-done | bytes 327712 | tf_op jit(solution)/shard_map/ppermute | solution.py:25
  133.7 2.3 collective-permute-done.12
  136.0 3.1 collective-permute-start.17
  142.7 4.5 %collective-permute-done.14 = bf16[256,640]{1,0:T(8,128)(2,1)S(1)} collective-permute-done((bf16[256,640]{1,0:T(8,128)(2,1)S(1)}, bf16[256,640]{1,0:T(8,128)(2,1)S(1)}, u32[]{:S(2)}, u32[]{:S(2)}) %collective-permute-start.14) | collective-permute-done | bytes 327712 | tf_op jit(solution)/shard_map/ppermute | solution.py:25
  149.2 3.0 collective-permute-done.15
  153.0 3.8 collective-permute-done.16
  158.3 2.9 gather_fusion
  161.3 3.5 reshape.150
  164.8 3.5 copy.99
  171.7 4.3 %gather_fusion.1 = bf16[12,128,640]{2,1,0:T(8,128)(2,1)} fusion(bf16[22,128,640]{2,1,0:T(8,128)(2,1)} %bitcast.87, s32[1024]{0:T(1024)S(1)} %pad_clamp_fusion), kind=kCustom, calls=%fused_computation.1 | custom fusion | bytes 3932208 | tf_op jit(solution)/shard_map/gather | solution.py:55
  175.9 5.6 %reshape.151 = bf16[2,768,5,128]{3,2,1,0:T(8,128)(2,1)} reshape(bf16[12,128,640]{2,1,0:T(8,128)(2,1)} %gather_fusion.1) | data formatting | bytes 3932160 | tf_op jit(solution)/shard_map/reshape | solution.py:55
  184.3 2.1 multiply_reduce_fusion.1
  186.5 9.6 %all-gather.1 = f32[8,2,128]{2,1,0:T(2,128)S(1)} all-gather(f32[1,2,128]{2,1,0:T(2,128)S(1)} %bitcast.91), channel_id=2, replica_groups=mesh['frame'=32,'head'=8] {'head'}, dimensions={0}, use_global_device_ids=true | all-gather | bytes 9216 | tf_op jit(solution)/shard_map/all_gather | solution.py:15
  197.5 4.9 %convolution_bitcast_fusion = f32[2,768,5,128]{1,3,2,0:T(8,128)} fusion(bf16[2,128,5,128]{1,3,2,0:T(8,128)(2,1)S(1)} %get-tuple-element.16, f32[2,5,128,768]{2,3,1,0:T(8,128)} %copy-done.21, f32[2,5,128]{2,1,0:T(8,128)S(1)} %get-tuple-element.41), kind=kOutput, calls=%fused_computation.10 | convolution fusion | flops 253624320 | bytes 8197120 | tf_op jit(solution)/shard_map/bhqk,bqhd->bkhd/dot_general | solution.py:94
  205.3 5.0 %copy.103 = f32[2,768,5,128]{3,2,1,0:T(8,128)} copy(f32[2,768,5,128]{3,1,2,0:T(8,128)S(1)} %multiply_bitcast_fusion) | data formatting | bytes 7864320 | tf_op jit(solution)/shard_map/mul | solution.py:91
  210.3 5.4 %reshape.116 = f32[12,81920]{1,0:T(8,128)} reshape(f32[2,768,5,128]{3,2,1,0:T(8,128)} %copy.103) | data formatting | bytes 7864320 | tf_op jit(solution)/shard_map/reshape | solution.py:95
  215.7 9.0 %fusion.48 = (bf16[22,81920]{1,0:T(8,128)(2,1)S(1)}, f32[22,81920]{1,0:T(8,128)}) fusion(f32[12,81920]{1,0:T(8,128)} %reshape.116, s32[12]{0:T(128)S(1)} %eq.75), kind=kOutput, calls=%fused_computation.109 | convolution fusion | flops 261325056 | bytes 14745648 | tf_op jit(solution)/shard_map/dot_general | solution.py:101
  224.7 3.8 fusion.46
  231.1 15.7 %collective-permute-start.27 = (bf16[2,81920]{1,0:T(2,128)(2,1)}, bf16[2,81920]{1,0:T(2,128)(2,1)S(1)}, u32[]{:S(2)}, u32[]{:S(2)}) collective-permute-start(bf16[2,81920]{1,0:T(2,128)(2,1)} %get-tuple-element.34), channel_id=1, source_target_pairs={{0,64},{8,72},{16,80},{24,88},{32,96},{40,104},{48,112},{56,120},{... | collective-permute-start | bytes 983048 | tf_op jit(solution)/shard_map/ppermute | solution.py:25
  248.7 11.5 %collective-permute-start.25 = (bf16[2,81920]{1,0:T(2,128)(2,1)}, bf16[2,81920]{1,0:T(2,128)(2,1)}, u32[]{:S(2)}, u32[]{:S(2)}) collective-permute-start(bf16[2,81920]{1,0:T(2,128)(2,1)} %get-tuple-element.36), channel_id=1, source_target_pairs={{0,32},{8,40},{16,48},{24,56},{32,64},{40,72},{48,80},{56,88},{64,... | collective-permute-start | bytes 983048 | tf_op jit(solution)/shard_map/ppermute | solution.py:25
  260.2 6.0 %copy.105 = f32[2,768,5,128]{3,2,1,0:T(8,128)} copy(f32[2,768,5,128]{1,3,2,0:T(8,128)} %convolution_bitcast_fusion) | data formatting | bytes 7864320 | tf_op jit(solution)/shard_map/bhqk,bqhd->bkhd/transpose | solution.py:94
  266.2 5.3 %reshape.117 = f32[12,81920]{1,0:T(8,128)} reshape(f32[2,768,5,128]{3,2,1,0:T(8,128)} %copy.105) | data formatting | bytes 7864320 | tf_op jit(solution)/shard_map/reshape | solution.py:96
  271.5 9.1 %fusion.49 = (bf16[22,81920]{1,0:T(8,128)(2,1)S(1)}, f32[22,81920]{1,0:T(8,128)}) fusion(f32[12,81920]{1,0:T(8,128)} %reshape.117, s32[12]{0:T(128)S(1)} %eq.75), kind=kOutput, calls=%fused_computation.110 | convolution fusion | flops 261325056 | bytes 14745648 | tf_op jit(solution)/shard_map/dot_general | solution.py:104
  280.6 2.1 collective-permute-start.24
  282.7 13.0 %collective-permute-start.23 = (bf16[2,81920]{1,0:T(2,128)(2,1)S(1)}, bf16[2,81920]{1,0:T(2,128)(2,1)S(1)}, u32[]{:S(2)}, u32[]{:S(2)}) collective-permute-start(bf16[2,81920]{1,0:T(2,128)(2,1)S(1)} %copy-done.14), channel_id=1, source_target_pairs={{0,16},{8,24},{16,32},{24,40},{32,48},{40,56},{48,64},{56,72},{64,... | collective-permute-start | bytes 983048 | tf_op jit(solution)/shard_map/ppermute | solution.py:25
  297.7 13.4 %collective-permute-start.21 = (bf16[2,81920]{1,0:T(2,128)(2,1)S(1)}, bf16[2,81920]{1,0:T(2,128)(2,1)S(1)}, u32[]{:S(2)}, u32[]{:S(2)}) collective-permute-start(bf16[2,81920]{1,0:T(2,128)(2,1)S(1)} %copy-done.12), channel_id=1, source_target_pairs={{0,8},{8,16},{16,24},{24,32},{32,40},{40,48},{48,56},{56,64},{64,7... | collective-permute-start | bytes 983048 | tf_op jit(solution)/shard_map/ppermute | solution.py:25
  313.0 3.8 fusion.45
  316.8 2.0 collective-permute-start.39
  323.2 12.5 %collective-permute-done.21 = bf16[2,81920]{1,0:T(2,128)(2,1)S(1)} collective-permute-done((bf16[2,81920]{1,0:T(2,128)(2,1)S(1)}, bf16[2,81920]{1,0:T(2,128)(2,1)S(1)}, u32[]{:S(2)}, u32[]{:S(2)}) %collective-permute-start.21) | collective-permute-done | bytes 327712 | tf_op jit(solution)/shard_map/ppermute | solution.py:25
  341.9 12.3 %collective-permute-done.39 = bf16[2,81920]{1,0:T(2,128)(2,1)} collective-permute-done((bf16[2,81920]{1,0:T(2,128)(2,1)}, bf16[2,81920]{1,0:T(2,128)(2,1)}, u32[]{:S(2)}, u32[]{:S(2)}) %collective-permute-start.39) | collective-permute-done | bytes 327712 | tf_op jit(solution)/shard_map/ppermute | solution.py:25
  358.1 10.2 %collective-permute-done.37 = bf16[2,81920]{1,0:T(2,128)(2,1)} collective-permute-done((bf16[2,81920]{1,0:T(2,128)(2,1)}, bf16[2,81920]{1,0:T(2,128)(2,1)}, u32[]{:S(2)}, u32[]{:S(2)}) %collective-permute-start.37) | collective-permute-done | bytes 327712 | tf_op jit(solution)/shard_map/ppermute | solution.py:25
  370.2 10.1 %collective-permute-start.31 = (bf16[2,81920]{1,0:T(2,128)(2,1)}, bf16[2,81920]{1,0:T(2,128)(2,1)S(1)}, u32[]{:S(2)}, u32[]{:S(2)}) collective-permute-start(bf16[2,81920]{1,0:T(2,128)(2,1)} %get-tuple-element.30), channel_id=1, source_target_pairs={{0,8},{8,16},{16,24},{24,32},{32,40},{40,48},{48,56},{56,64},{64,7... | collective-permute-start | bytes 983048 | tf_op jit(solution)/shard_map/ppermute | solution.py:25
  380.3 2.2 collective-permute-start.30
  382.5 4.1 %add_convert_fusion.1 = bf16[2,81920]{1,0:T(2,128)(2,1)S(1)} fusion(bf16[2,81920]{1,0:T(2,128)(2,1)S(1)} %collective-permute-done.29, bf16[2,81920]{1,0:T(2,128)(2,1)S(1)} %collective-permute-done.28, bf16[2,81920]{1,0:T(2,128)(2,1)S(1)} %collective-permute-done.27, bf16[2,81920]{1,0:T(2,128)(2,1)} %copy-done.5, ...), kind=kLoop, calls=%fused_computation.35 | loop fusion | flops 3440640 | bytes 4259840 | tf_op jit(solution)/shard_map/convert_element_type | solution.py:118
  389.4 4.2 %collective-permute-done.31 = bf16[2,81920]{1,0:T(2,128)(2,1)S(1)} collective-permute-done((bf16[2,81920]{1,0:T(2,128)(2,1)}, bf16[2,81920]{1,0:T(2,128)(2,1)S(1)}, u32[]{:S(2)}, u32[]{:S(2)}) %collective-permute-start.31) | collective-permute-done | bytes 327712 | tf_op jit(solution)/shard_map/ppermute | solution.py:25
  393.6 14.5 %collective-permute-done.30 = bf16[2,81920]{1,0:T(2,128)(2,1)S(1)} collective-permute-done((bf16[2,81920]{1,0:T(2,128)(2,1)}, bf16[2,81920]{1,0:T(2,128)(2,1)S(1)}, u32[]{:S(2)}, u32[]{:S(2)}) %collective-permute-start.30) | collective-permute-done | bytes 327712 | tf_op jit(solution)/shard_map/ppermute | solution.py:25
  408.0 4.0 add_convert_fusion
  (145 shorter events, 86.5 us)
Async XLA Ops:
  0.6 26.1 %copy-start.18 = (bf16[256,640]{1,0:T(8,128)(2,1)S(1)}, bf16[256,640]{1,0:T(8,128)(2,1)}, u32[]{:S(2)}) copy-start(bf16[256,640]{1,0:T(8,128)(2,1)} %param.9) | copy-start | bytes 983044
  0.6 26.9 %copy-start.16 = (bf16[256,640]{1,0:T(8,128)(2,1)S(1)}, bf16[256,640]{1,0:T(8,128)(2,1)}, u32[]{:S(2)}) copy-start(bf16[256,640]{1,0:T(8,128)(2,1)} %param.7) | copy-start | bytes 983044
  0.7 27.3 %copy-start.20 = (s32[64]{0:T(128)S(1)}, s32[64]{0:T(128)}, u32[]{:S(2)}) copy-start(s32[64]{0:T(128)} %param.13) | copy-start | bytes 772
  0.7 27.7 %copy-start.19 = (bf16[256,640]{1,0:T(8,128)(2,1)S(1)}, bf16[256,640]{1,0:T(8,128)(2,1)}, u32[]{:S(2)}) copy-start(bf16[256,640]{1,0:T(8,128)(2,1)} %param.10) | copy-start | bytes 983044
  0.7 36.5 %collective-permute-start = (bf16[256,640]{1,0:T(8,128)(2,1)}, bf16[256,640]{1,0:T(8,128)(2,1)}, u32[]{:S(2)}, u32[]{:S(2)}) collective-permute-start(bf16[256,640]{1,0:T(8,128)(2,1)} %param.8), channel_id=1, source_target_pairs={{0,8},{8,16},{16,24},{24,32},{32,40},{40,48},{48,56},{56,64},{64,7... | collective-permute-start | bytes 983048 | tf_op jit(solution)/shard_map/ppermute | solution.py:25
  7.7 35.3 %collective-permute-start.1 = (bf16[256,640]{1,0:T(8,128)(2,1)}, bf16[256,640]{1,0:T(8,128)(2,1)}, u32[]{:S(2)}, u32[]{:S(2)}) collective-permute-start(bf16[256,640]{1,0:T(8,128)(2,1)} %param.8), channel_id=1, source_target_pairs={{8,0},{16,8},{24,16},{32,24},{40,32},{48,40},{56,48},{64,56},{72,6... | collective-permute-start | bytes 983048 | tf_op jit(solution)/shard_map/ppermute | solution.py:25
  9.6 48.4 %collective-permute-start.2 = (bf16[256,640]{1,0:T(8,128)(2,1)}, bf16[256,640]{1,0:T(8,128)(2,1)}, u32[]{:S(2)}, u32[]{:S(2)}) collective-permute-start(bf16[256,640]{1,0:T(8,128)(2,1)} %param.8), channel_id=1, source_target_pairs={{0,16},{8,24},{16,32},{24,40},{32,48},{40,56},{48,64},{56,72},{64,... | collective-permute-start | bytes 983048 | tf_op jit(solution)/shard_map/ppermute | solution.py:25
  14.5 47.3 %collective-permute-start.3 = (bf16[256,640]{1,0:T(8,128)(2,1)}, bf16[256,640]{1,0:T(8,128)(2,1)}, u32[]{:S(2)}, u32[]{:S(2)}) collective-permute-start(bf16[256,640]{1,0:T(8,128)(2,1)} %param.8), channel_id=1, source_target_pairs={{16,0},{24,8},{32,16},{40,24},{48,32},{56,40},{64,48},{72,56},{80,... | collective-permute-start | bytes 983048 | tf_op jit(solution)/shard_map/ppermute | solution.py:25
  17.0 50.6 %collective-permute-start.4 = (bf16[256,640]{1,0:T(8,128)(2,1)}, bf16[256,640]{1,0:T(8,128)(2,1)}, u32[]{:S(2)}, u32[]{:S(2)}) collective-permute-start(bf16[256,640]{1,0:T(8,128)(2,1)} %param.8), channel_id=1, source_target_pairs={{0,32},{8,40},{16,48},{24,56},{32,64},{40,72},{48,80},{56,88},{64,... | collective-permute-start | bytes 983048 | tf_op jit(solution)/shard_map/ppermute | solution.py:25
  37.1 33.4 %collective-permute-start.5 = (bf16[256,640]{1,0:T(8,128)(2,1)S(1)}, bf16[256,640]{1,0:T(8,128)(2,1)S(1)}, u32[]{:S(2)}, u32[]{:S(2)}) collective-permute-start(bf16[256,640]{1,0:T(8,128)(2,1)S(1)} %copy-done.17), channel_id=1, source_target_pairs={{32,0},{40,8},{48,16},{56,24},{64,32},{72,40},{80,48},{88,56},{96,... | collective-permute-start | bytes 983048 | tf_op jit(solution)/shard_map/ppermute | solution.py:25
  43.0 44.3 %collective-permute-start.6 = (bf16[256,640]{1,0:T(8,128)(2,1)S(1)}, bf16[256,640]{1,0:T(8,128)(2,1)S(1)}, u32[]{:S(2)}, u32[]{:S(2)}) collective-permute-start(bf16[256,640]{1,0:T(8,128)(2,1)S(1)} %copy-done.17), channel_id=1, source_target_pairs={{0,64},{8,72},{16,80},{24,88},{32,96},{40,104},{48,112},{56,120},{... | collective-permute-start | bytes 983048 | tf_op jit(solution)/shard_map/ppermute | solution.py:25
  58.1 31.9 %collective-permute-start.7 = (bf16[256,640]{1,0:T(8,128)(2,1)S(1)}, bf16[256,640]{1,0:T(8,128)(2,1)S(1)}, u32[]{:S(2)}, u32[]{:S(2)}) collective-permute-start(bf16[256,640]{1,0:T(8,128)(2,1)S(1)} %copy-done.17), channel_id=1, source_target_pairs={{64,0},{72,8},{80,16},{88,24},{96,32},{104,40},{112,48},{120,56},{... | collective-permute-start | bytes 983048 | tf_op jit(solution)/shard_map/ppermute | solution.py:25
  61.7 36.6 %collective-permute-start.8 = (bf16[256,640]{1,0:T(8,128)(2,1)S(1)}, bf16[256,640]{1,0:T(8,128)(2,1)S(1)}, u32[]{:S(2)}, u32[]{:S(2)}) collective-permute-start(bf16[256,640]{1,0:T(8,128)(2,1)S(1)} %copy-done.17), channel_id=1, source_target_pairs={{0,128},{8,136},{16,144},{24,152},{32,160},{40,168},{48,176},{56,1... | collective-permute-start | bytes 983048 | tf_op jit(solution)/shard_map/ppermute | solution.py:25
  67.5 33.5 %collective-permute-start.9 = (bf16[256,640]{1,0:T(8,128)(2,1)S(1)}, bf16[256,640]{1,0:T(8,128)(2,1)S(1)}, u32[]{:S(2)}, u32[]{:S(2)}) collective-permute-start(bf16[256,640]{1,0:T(8,128)(2,1)S(1)} %copy-done.17), channel_id=1, source_target_pairs={{128,0},{136,8},{144,16},{152,24},{160,32},{168,40},{176,48},{184,... | collective-permute-start | bytes 983048 | tf_op jit(solution)/shard_map/ppermute | solution.py:25
  70.6 57.8 %collective-permute-start.10 = (bf16[256,640]{1,0:T(8,128)(2,1)S(1)}, bf16[256,640]{1,0:T(8,128)(2,1)S(1)}, u32[]{:S(2)}, u32[]{:S(2)}) collective-permute-start(bf16[256,640]{1,0:T(8,128)(2,1)S(1)} %copy-done.18), channel_id=1, source_target_pairs={{0,8},{8,16},{16,24},{24,32},{32,40},{40,48},{48,56},{56,64},{64,7... | collective-permute-start | bytes 983048 | tf_op jit(solution)/shard_map/ppermute | solution.py:25
  87.3 43.8 %collective-permute-start.11 = (bf16[256,640]{1,0:T(8,128)(2,1)S(1)}, bf16[256,640]{1,0:T(8,128)(2,1)S(1)}, u32[]{:S(2)}, u32[]{:S(2)}) collective-permute-start(bf16[256,640]{1,0:T(8,128)(2,1)S(1)} %copy-done.18), channel_id=1, source_target_pairs={{8,0},{16,8},{24,16},{32,24},{40,32},{48,40},{56,48},{64,56},{72,6... | collective-permute-start | bytes 983048 | tf_op jit(solution)/shard_map/ppermute | solution.py:25
  90.0 46.1 %collective-permute-start.12 = (bf16[256,640]{1,0:T(8,128)(2,1)S(1)}, bf16[256,640]{1,0:T(8,128)(2,1)S(1)}, u32[]{:S(2)}, u32[]{:S(2)}) collective-permute-start(bf16[256,640]{1,0:T(8,128)(2,1)S(1)} %copy-done.18), channel_id=1, source_target_pairs={{0,16},{8,24},{16,32},{24,40},{32,48},{40,56},{48,64},{56,72},{64,... | collective-permute-start | bytes 983048 | tf_op jit(solution)/shard_map/ppermute | solution.py:25
  98.4 41.5 %collective-permute-start.13 = (bf16[256,640]{1,0:T(8,128)(2,1)S(1)}, bf16[256,640]{1,0:T(8,128)(2,1)S(1)}, u32[]{:S(2)}, u32[]{:S(2)}) collective-permute-start(bf16[256,640]{1,0:T(8,128)(2,1)S(1)} %copy-done.18), channel_id=1, source_target_pairs={{16,0},{24,8},{32,16},{40,24},{48,32},{56,40},{64,48},{72,56},{80,... | collective-permute-start | bytes 983048 | tf_op jit(solution)/shard_map/ppermute | solution.py:25
  101.0 46.2 %collective-permute-start.14 = (bf16[256,640]{1,0:T(8,128)(2,1)S(1)}, bf16[256,640]{1,0:T(8,128)(2,1)S(1)}, u32[]{:S(2)}, u32[]{:S(2)}) collective-permute-start(bf16[256,640]{1,0:T(8,128)(2,1)S(1)} %copy-done.18), channel_id=1, source_target_pairs={{0,32},{8,40},{16,48},{24,56},{32,64},{40,72},{48,80},{56,88},{64,... | collective-permute-start | bytes 983048 | tf_op jit(solution)/shard_map/ppermute | solution.py:25
  128.3 23.9 %collective-permute-start.15 = (bf16[256,640]{1,0:T(8,128)(2,1)S(1)}, bf16[256,640]{1,0:T(8,128)(2,1)S(1)}, u32[]{:S(2)}, u32[]{:S(2)}) collective-permute-start(bf16[256,640]{1,0:T(8,128)(2,1)S(1)} %copy-done.18), channel_id=1, source_target_pairs={{32,0},{40,8},{48,16},{56,24},{64,32},{72,40},{80,48},{88,56},{96,... | collective-permute-start | bytes 983048 | tf_op jit(solution)/shard_map/ppermute | solution.py:25
  131.0 25.8 %collective-permute-start.16 = (bf16[256,640]{1,0:T(8,128)(2,1)S(1)}, bf16[256,640]{1,0:T(8,128)(2,1)S(1)}, u32[]{:S(2)}, u32[]{:S(2)}) collective-permute-start(bf16[256,640]{1,0:T(8,128)(2,1)S(1)} %copy-done.18), channel_id=1, source_target_pairs={{0,64},{8,72},{16,80},{24,88},{32,96},{40,104},{48,112},{56,120},{... | collective-permute-start | bytes 983048 | tf_op jit(solution)/shard_map/ppermute | solution.py:25
  136.0 21.5 %collective-permute-start.17 = (bf16[256,640]{1,0:T(8,128)(2,1)S(1)}, bf16[256,640]{1,0:T(8,128)(2,1)S(1)}, u32[]{:S(2)}, u32[]{:S(2)}) collective-permute-start(bf16[256,640]{1,0:T(8,128)(2,1)S(1)} %copy-done.18), channel_id=1, source_target_pairs={{64,0},{72,8},{80,16},{88,24},{96,32},{104,40},{112,48},{120,56},{... | collective-permute-start | bytes 983048 | tf_op jit(solution)/shard_map/ppermute | solution.py:25
  139.9 28.3 %collective-permute-start.18 = (bf16[256,640]{1,0:T(8,128)(2,1)S(1)}, bf16[256,640]{1,0:T(8,128)(2,1)}, u32[]{:S(2)}, u32[]{:S(2)}) collective-permute-start(bf16[256,640]{1,0:T(8,128)(2,1)S(1)} %copy-done.18), channel_id=1, source_target_pairs={{0,128},{8,136},{16,144},{24,152},{32,160},{40,168},{48,176},{56,1... | collective-permute-start | bytes 983048 | tf_op jit(solution)/shard_map/ppermute | solution.py:25
  147.2 22.8 %collective-permute-start.19 = (bf16[256,640]{1,0:T(8,128)(2,1)S(1)}, bf16[256,640]{1,0:T(8,128)(2,1)}, u32[]{:S(2)}, u32[]{:S(2)}) collective-permute-start(bf16[256,640]{1,0:T(8,128)(2,1)S(1)} %copy-done.18), channel_id=1, source_target_pairs={{128,0},{136,8},{144,16},{152,24},{160,32},{168,40},{176,48},{184,... | collective-permute-start | bytes 983048 | tf_op jit(solution)/shard_map/ppermute | solution.py:25
  228.5 52.2 %collective-permute-start.29 = (bf16[2,81920]{1,0:T(2,128)(2,1)}, bf16[2,81920]{1,0:T(2,128)(2,1)S(1)}, u32[]{:S(2)}, u32[]{:S(2)}) collective-permute-start(bf16[2,81920]{1,0:T(2,128)(2,1)} %get-tuple-element.32), channel_id=1, source_target_pairs={{0,128},{8,136},{16,144},{24,152},{32,160},{40,168},{48,176},{56,1... | collective-permute-start | bytes 983048 | tf_op jit(solution)/shard_map/ppermute | solution.py:25
  229.8 52.9 %collective-permute-start.28 = (bf16[2,81920]{1,0:T(2,128)(2,1)}, bf16[2,81920]{1,0:T(2,128)(2,1)S(1)}, u32[]{:S(2)}, u32[]{:S(2)}) collective-permute-start(bf16[2,81920]{1,0:T(2,128)(2,1)} %get-tuple-element.33), channel_id=1, source_target_pairs={{128,0},{136,8},{144,16},{152,24},{160,32},{168,40},{176,48},{184,... | collective-permute-start | bytes 983048 | tf_op jit(solution)/shard_map/ppermute | solution.py:25
  231.1 64.6 %collective-permute-start.27 = (bf16[2,81920]{1,0:T(2,128)(2,1)}, bf16[2,81920]{1,0:T(2,128)(2,1)S(1)}, u32[]{:S(2)}, u32[]{:S(2)}) collective-permute-start(bf16[2,81920]{1,0:T(2,128)(2,1)} %get-tuple-element.34), channel_id=1, source_target_pairs={{0,64},{8,72},{16,80},{24,88},{32,96},{40,104},{48,112},{56,120},{... | collective-permute-start | bytes 983048 | tf_op jit(solution)/shard_map/ppermute | solution.py:25
  246.7 50.9 %collective-permute-start.26 = (bf16[2,81920]{1,0:T(2,128)(2,1)}, bf16[2,81920]{1,0:T(2,128)(2,1)S(1)}, u32[]{:S(2)}, u32[]{:S(2)}) collective-permute-start(bf16[2,81920]{1,0:T(2,128)(2,1)} %get-tuple-element.35), channel_id=1, source_target_pairs={{64,0},{72,8},{80,16},{88,24},{96,32},{104,40},{112,48},{120,56},{... | collective-permute-start | bytes 983048 | tf_op jit(solution)/shard_map/ppermute | solution.py:25
  248.7 62.3 %collective-permute-start.25 = (bf16[2,81920]{1,0:T(2,128)(2,1)}, bf16[2,81920]{1,0:T(2,128)(2,1)}, u32[]{:S(2)}, u32[]{:S(2)}) collective-permute-start(bf16[2,81920]{1,0:T(2,128)(2,1)} %get-tuple-element.36), channel_id=1, source_target_pairs={{0,32},{8,40},{16,48},{24,56},{32,64},{40,72},{48,80},{56,88},{64,... | collective-permute-start | bytes 983048 | tf_op jit(solution)/shard_map/ppermute | solution.py:25
  271.5 26.2 %copy-start.12 = (bf16[2,81920]{1,0:T(2,128)(2,1)S(1)}, bf16[2,81920]{1,0:T(2,128)(2,1)}, u32[]{:S(2)}) copy-start(bf16[2,81920]{1,0:T(2,128)(2,1)} %get-tuple-element.40) | copy-start | bytes 983044
  271.5 39.5 %copy-start.10 = (bf16[2,81920]{1,0:T(2,128)(2,1)S(1)}, bf16[2,81920]{1,0:T(2,128)(2,1)}, u32[]{:S(2)}) copy-start(bf16[2,81920]{1,0:T(2,128)(2,1)} %get-tuple-element.31) | copy-start | bytes 983044
  280.6 59.5 %copy-start.1 = (bf16[2,5,128,768]{2,3,1,0:T(8,128)(2,1)S(1)}, bf16[2,5,128,768]{2,3,1,0:T(8,128)(2,1)}, u32[]{:S(2)}) copy-start(bf16[2,5,128,768]{2,3,1,0:T(8,128)(2,1)} %copy-done) | copy-start | bytes 5898244
  280.6 36.2 %collective-permute-start.24 = (bf16[2,81920]{1,0:T(2,128)(2,1)S(1)}, bf16[2,81920]{1,0:T(2,128)(2,1)S(1)}, u32[]{:S(2)}, u32[]{:S(2)}) collective-permute-start(bf16[2,81920]{1,0:T(2,128)(2,1)S(1)} %copy-done.15), channel_id=1, source_target_pairs={{32,0},{40,8},{48,16},{56,24},{64,32},{72,40},{80,48},{88,56},{96,... | collective-permute-start | bytes 983048 | tf_op jit(solution)/shard_map/ppermute | solution.py:25
  282.7 36.1 %collective-permute-start.23 = (bf16[2,81920]{1,0:T(2,128)(2,1)S(1)}, bf16[2,81920]{1,0:T(2,128)(2,1)S(1)}, u32[]{:S(2)}, u32[]{:S(2)}) collective-permute-start(bf16[2,81920]{1,0:T(2,128)(2,1)S(1)} %copy-done.14), channel_id=1, source_target_pairs={{0,16},{8,24},{16,32},{24,40},{32,48},{40,56},{48,64},{56,72},{64,... | collective-permute-start | bytes 983048 | tf_op jit(solution)/shard_map/ppermute | solution.py:25
  295.7 25.6 %collective-permute-start.22 = (bf16[2,81920]{1,0:T(2,128)(2,1)S(1)}, bf16[2,81920]{1,0:T(2,128)(2,1)S(1)}, u32[]{:S(2)}, u32[]{:S(2)}) collective-permute-start(bf16[2,81920]{1,0:T(2,128)(2,1)S(1)} %copy-done.13), channel_id=1, source_target_pairs={{16,0},{24,8},{32,16},{40,24},{48,32},{56,40},{64,48},{72,56},{80,... | collective-permute-start | bytes 983048 | tf_op jit(solution)/shard_map/ppermute | solution.py:25
  297.6 40.5 %copy-start.5 = (bf16[2,81920]{1,0:T(2,128)(2,1)}, bf16[2,81920]{1,0:T(2,128)(2,1)S(1)}, u32[]{:S(2)}) copy-start(bf16[2,81920]{1,0:T(2,128)(2,1)S(1)} %collective-permute-done.26) | copy-start | bytes 983044
  297.7 38.1 %collective-permute-start.21 = (bf16[2,81920]{1,0:T(2,128)(2,1)S(1)}, bf16[2,81920]{1,0:T(2,128)(2,1)S(1)}, u32[]{:S(2)}, u32[]{:S(2)}) collective-permute-start(bf16[2,81920]{1,0:T(2,128)(2,1)S(1)} %copy-done.12), channel_id=1, source_target_pairs={{0,8},{8,16},{16,24},{24,32},{32,40},{40,48},{48,56},{56,64},{64,7... | collective-permute-start | bytes 983048 | tf_op jit(solution)/shard_map/ppermute | solution.py:25
  311.0 27.1 %collective-permute-start.20 = (bf16[2,81920]{1,0:T(2,128)(2,1)S(1)}, bf16[2,81920]{1,0:T(2,128)(2,1)S(1)}, u32[]{:S(2)}, u32[]{:S(2)}) collective-permute-start(bf16[2,81920]{1,0:T(2,128)(2,1)S(1)} %copy-done.10), channel_id=1, source_target_pairs={{8,0},{16,8},{24,16},{32,24},{40,32},{48,40},{56,48},{64,56},{72,6... | collective-permute-start | bytes 983048 | tf_op jit(solution)/shard_map/ppermute | solution.py:25
  316.8 37.5 %collective-permute-start.39 = (bf16[2,81920]{1,0:T(2,128)(2,1)}, bf16[2,81920]{1,0:T(2,128)(2,1)}, u32[]{:S(2)}, u32[]{:S(2)}) collective-permute-start(bf16[2,81920]{1,0:T(2,128)(2,1)} %get-tuple-element.22), channel_id=1, source_target_pairs={{0,128},{8,136},{16,144},{24,152},{32,160},{40,168},{48,176},{56,1... | collective-permute-start | bytes 983048 | tf_op jit(solution)/shard_map/ppermute | solution.py:25
  318.8 37.3 %collective-permute-start.38 = (bf16[2,81920]{1,0:T(2,128)(2,1)}, bf16[2,81920]{1,0:T(2,128)(2,1)}, u32[]{:S(2)}, u32[]{:S(2)}) collective-permute-start(bf16[2,81920]{1,0:T(2,128)(2,1)} %get-tuple-element.23), channel_id=1, source_target_pairs={{128,0},{136,8},{144,16},{152,24},{160,32},{168,40},{176,48},{184,... | collective-permute-start | bytes 983048 | tf_op jit(solution)/shard_map/ppermute | solution.py:25
  321.3 47.0 %collective-permute-start.37 = (bf16[2,81920]{1,0:T(2,128)(2,1)}, bf16[2,81920]{1,0:T(2,128)(2,1)}, u32[]{:S(2)}, u32[]{:S(2)}) collective-permute-start(bf16[2,81920]{1,0:T(2,128)(2,1)} %get-tuple-element.24), channel_id=1, source_target_pairs={{0,64},{8,72},{16,80},{24,88},{32,96},{40,104},{48,112},{56,120},{... | collective-permute-start | bytes 983048 | tf_op jit(solution)/shard_map/ppermute | solution.py:25
  335.7 34.5 %collective-permute-start.36 = (bf16[2,81920]{1,0:T(2,128)(2,1)}, bf16[2,81920]{1,0:T(2,128)(2,1)}, u32[]{:S(2)}, u32[]{:S(2)}) collective-permute-start(bf16[2,81920]{1,0:T(2,128)(2,1)} %get-tuple-element.25), channel_id=1, source_target_pairs={{64,0},{72,8},{80,16},{88,24},{96,32},{104,40},{112,48},{120,56},{... | collective-permute-start | bytes 983048 | tf_op jit(solution)/shard_map/ppermute | solution.py:25
  338.2 42.1 %collective-permute-start.35 = (bf16[2,81920]{1,0:T(2,128)(2,1)}, bf16[2,81920]{1,0:T(2,128)(2,1)}, u32[]{:S(2)}, u32[]{:S(2)}) collective-permute-start(bf16[2,81920]{1,0:T(2,128)(2,1)} %get-tuple-element.26), channel_id=1, source_target_pairs={{0,32},{8,40},{16,48},{24,56},{32,64},{40,72},{48,80},{56,88},{64,... | collective-permute-start | bytes 983048 | tf_op jit(solution)/shard_map/ppermute | solution.py:25
  354.2 33.3 %collective-permute-start.34 = (bf16[2,81920]{1,0:T(2,128)(2,1)}, bf16[2,81920]{1,0:T(2,128)(2,1)S(1)}, u32[]{:S(2)}, u32[]{:S(2)}) collective-permute-start(bf16[2,81920]{1,0:T(2,128)(2,1)} %get-tuple-element.27), channel_id=1, source_target_pairs={{32,0},{40,8},{48,16},{56,24},{64,32},{72,40},{80,48},{88,56},{96,... | collective-permute-start | bytes 983048 | tf_op jit(solution)/shard_map/ppermute | solution.py:25
  356.2 33.2 %collective-permute-start.33 = (bf16[2,81920]{1,0:T(2,128)(2,1)}, bf16[2,81920]{1,0:T(2,128)(2,1)S(1)}, u32[]{:S(2)}, u32[]{:S(2)}) collective-permute-start(bf16[2,81920]{1,0:T(2,128)(2,1)} %get-tuple-element.28), channel_id=1, source_target_pairs={{0,16},{8,24},{16,32},{24,40},{32,48},{40,56},{48,64},{56,72},{64,... | collective-permute-start | bytes 983048 | tf_op jit(solution)/shard_map/ppermute | solution.py:25
  368.3 21.1 %collective-permute-start.32 = (bf16[2,81920]{1,0:T(2,128)(2,1)}, bf16[2,81920]{1,0:T(2,128)(2,1)S(1)}, u32[]{:S(2)}, u32[]{:S(2)}) collective-permute-start(bf16[2,81920]{1,0:T(2,128)(2,1)} %get-tuple-element.29), channel_id=1, source_target_pairs={{16,0},{24,8},{32,16},{40,24},{48,32},{56,40},{64,48},{72,56},{80,... | collective-permute-start | bytes 983048 | tf_op jit(solution)/shard_map/ppermute | solution.py:25
  370.2 23.3 %collective-permute-start.31 = (bf16[2,81920]{1,0:T(2,128)(2,1)}, bf16[2,81920]{1,0:T(2,128)(2,1)S(1)}, u32[]{:S(2)}, u32[]{:S(2)}) collective-permute-start(bf16[2,81920]{1,0:T(2,128)(2,1)} %get-tuple-element.30), channel_id=1, source_target_pairs={{0,8},{8,16},{16,24},{24,32},{32,40},{40,48},{48,56},{56,64},{64,7... | collective-permute-start | bytes 983048 | tf_op jit(solution)/shard_map/ppermute | solution.py:25
  380.3 27.8 %collective-permute-start.30 = (bf16[2,81920]{1,0:T(2,128)(2,1)}, bf16[2,81920]{1,0:T(2,128)(2,1)S(1)}, u32[]{:S(2)}, u32[]{:S(2)}) collective-permute-start(bf16[2,81920]{1,0:T(2,128)(2,1)} %get-tuple-element.21), channel_id=1, source_target_pairs={{8,0},{16,8},{24,16},{32,24},{40,32},{48,40},{56,48},{64,56},{72,6... | collective-permute-start | bytes 983048 | tf_op jit(solution)/shard_map/ppermute | solution.py:25
  (15 other events, 144.8 us)
